TPU v7x, 256 devices: a whole 4x4x8 slice. The times are simulated.
256 devices in a mesh: dp: 16 (over y_lo, x, core), seq: 16 (over z, y_hi).
Axes of the slice: x: 4, y: 4 (y_hi: 2, y_lo: 2; y = y_hi * 2 + y_lo), z: 8, core: 2. Of those that a mesh axis runs over, the one named last changes fastest.
Arguments:
- student_in: bfloat16 [32768, 3584], P(('dp', 'seq')), may hold values from -24 to 24
- weight: bfloat16 [3584, 512], P(('dp', 'seq')), may hold values from -0.09375 to 0.09375
- queries: bfloat16 [32768, 512], P(('dp', 'seq')), may hold values from -8 to 8, as said below
- keys: bfloat16 [32768, 128], P(('dp', 'seq')), may hold values from -8 to 8
- values: bfloat16 [32768, 128], P(('dp', 'seq')), may hold values from -6 to 6
- lengths: int32 [16, 4], P('dp'), may hold values from 1 to 1536, 2048 in all within a row
- assignment: int32 [16, 16], P('dp'), may hold values from 0 to 15, each once within a row
Outputs:
- attention: bfloat16 [32768, 512], P(('dp', 'seq'))
- weight_grad: float32 [3584, 512], P(('dp', 'seq'))
Inputs may be any that keep to these rules, and one draw needn't show every extreme that they name: `queries`: entries of head 0 and of keys may reach the ends of this range. Each row holds the lengths of 4 rollouts of one sequence, summing to 2048, the longest exactly 1536. `assignment`: each row is a permutation of the 16 rollout blocks of one sequence.
All inputs are finite; a program needn't handle non-finite values.
Results may differ from a plain program's by a relative error of at most 0.012.
Values may be sent and summed in bfloat16 or wider, within the bound.
No kernel may reach another device: no remote copies, remote signals or barrier semaphores. Data moves between devices by JAX's collectives and lax.ppermute only.
A program may use at most 64 MiB of HBM per device.

v0:
```python
import math
import jax
import jax.numpy as jnp
from jax import lax
from jax.sharding import PartitionSpec as P

HD = 128
HQ = 4
BLK = 128
EPSILON = 1e-06
NEGATIVE = -1e30


def side_by_side(arrays, axis, dim, along):
    both = jnp.concatenate(arrays, axis=along)
    whole, at, gathered = (lax.all_gather(both, axis, axis=dim, tiled=True), 0, [])
    for a in arrays:
        gathered.append(lax.slice_in_dim(whole, at, at + a.shape[along], axis=along))
        at += a.shape[along]
    return tuple(gathered)


def laid_out(tiles, dim):
    tiles = jnp.moveaxis(tiles, 0, dim)
    dims = tiles.shape
    return tiles.reshape(*dims[:dim], dims[dim] * dims[dim + 1], *dims[dim + 2 :])


def from_everyone(x, axis):
    copies = jnp.broadcast_to(x, (lax.axis_size(axis), *x.shape))
    return lax.all_to_all(copies, axis, split_axis=0, concat_axis=0, tiled=True)


def collect(x, axis, dim):
    return laid_out(from_everyone(x, axis), dim)


def in_blocks(x, dim, length):
    before, after = (x.shape[:dim], x.shape[dim + 1 :])
    return jnp.moveaxis(x.reshape(*before, length, -1, *after), dim, 0)


def sum_at_owner(x, axis, dim):
    tiles = in_blocks(x, dim, lax.axis_size(axis))
    arrived = lax.all_to_all(tiles, axis, split_axis=0, concat_axis=0, tiled=True)
    return arrived.astype(jnp.float32).sum(axis=0)


def locate(assign_row, doc_ends, first_slot, count):
    slot_ids = first_slot + jnp.arange(count, dtype=jnp.int32)
    block_ids = slot_ids // BLK
    block_table = jnp.arange(assign_row.shape[0], dtype=jnp.int32)
    placed = jnp.sum(
        jnp.where(block_ids[:, None] == block_table[None, :], assign_row[None, :], 0), axis=1
    )
    position = placed * BLK + slot_ids % BLK
    document = jnp.sum((position[:, None] >= doc_ends[None, :]).astype(jnp.int32), axis=1)
    return (position, document)


def absorb_block(state, key_block, value_block, query_heads, allowed):
    run_max, run_total, run_acc = state
    scores = jnp.einsum(
        "qhd,kd->hqk", query_heads, key_block, preferred_element_type=jnp.float32
    ) * HD ** (-0.5)
    masked = jnp.where(allowed[None], scores, NEGATIVE)
    new_max = jnp.maximum(run_max, jnp.max(masked, axis=-1))
    fading = jnp.exp(run_max - new_max)
    exp_terms = jnp.where(allowed[None], jnp.exp(masked - new_max[:, :, None]), 0.0)
    new_total = run_total * fading + jnp.sum(exp_terms, axis=-1)
    mixture = jnp.einsum(
        "hqk,kd->qhd",
        exp_terms.astype(jnp.bfloat16),
        value_block,
        preferred_element_type=jnp.float32,
    )
    new_acc = run_acc * fading.T[:, :, None] + mixture
    return (new_max, new_total, new_acc)


def local(student_in, weight, queries, keys, values, lengths, assignment):
    rows = queries.shape[0]
    assign_row = assignment[0]
    doc_ends = jnp.cumsum(lengths[0])
    query_pos, query_doc = locate(assign_row, doc_ends, lax.axis_index("seq") * rows, rows)
    query_heads = queries.reshape(rows, HQ, HD)
    start_state = (
        jnp.full((HQ, rows), NEGATIVE, jnp.float32),
        jnp.zeros((HQ, rows), jnp.float32),
        jnp.zeros((rows, HQ, HD), jnp.float32),
    )
    key_piece, value_piece = side_by_side((keys, values), "seq", 0, 1)
    count = key_piece.shape[0]
    step_rows = math.gcd(count, 512)
    steps_count = count // step_rows
    key_pos, key_doc = locate(assign_row, doc_ends, jnp.int32(0), count)

    def one_step(running, slabs):
        key_block, value_block, key_position, key_document = slabs
        allowed = (query_doc[:, None] == key_document[None, :]) & (
            query_pos[:, None] >= key_position[None, :]
        )
        updated = absorb_block(running, key_block, value_block, query_heads, allowed)
        return (updated, None)

    slabs = (
        key_piece.reshape(steps_count, step_rows, HD),
        value_piece.reshape(steps_count, step_rows, HD),
        key_pos.reshape(steps_count, step_rows),
        key_doc.reshape(steps_count, step_rows),
    )
    result, _ = lax.scan(one_step, start_state, slabs)
    final_max, final_total, final_acc = result
    attention = (final_acc / final_total.T[:, :, None]).reshape(rows, HQ * HD).astype(jnp.bfloat16)
    as_float = student_in.astype(jnp.float32)
    normed = (
        as_float * lax.rsqrt(jnp.mean(as_float * as_float, axis=1, keepdims=True) + EPSILON)
    ).astype(jnp.bfloat16)
    group_rows = collect(weight, "seq", 0)
    columns = normed
    predicted = jnp.dot(
        columns,
        lax.all_gather(group_rows, "dp", axis=0, tiled=True),
        preferred_element_type=jnp.float32,
    )
    dp_count = lax.axis_size("dp")
    seq_count = lax.axis_size("seq")
    token_total = rows * dp_count * seq_count
    scaled = ((predicted - attention.astype(jnp.float32)) * token_total ** (-0.5)).astype(
        jnp.bfloat16
    )
    columns = normed
    outer_rows = lax.psum_scatter(
        lax.dot_general(
            columns, scaled, (((0,), (0,)), ((), ())), preferred_element_type=jnp.float32
        ).astype(jnp.bfloat16),
        "dp",
        scatter_dimension=0,
        tiled=True,
    )
    weight_grad = sum_at_owner(outer_rows, "seq", 0)
    return (attention, weight_grad)


def solution(mesh):
    placed = (
        P(("dp", "seq"), None),
        P(("dp", "seq"), None),
        P(("dp", "seq"), None),
        P(("dp", "seq"), None),
        P(("dp", "seq"), None),
        P("dp", None),
        P("dp", None),
    )
    return jax.shard_map(
        local,
        mesh=mesh,
        in_specs=placed,
        out_specs=(P(("dp", "seq"), None), P(("dp", "seq"), None)),
        check_vma=False,
    )
```

profile of v0, /device:TPU:7, one launch (start us, length us, event | category | flops | bytes accessed | tf_op | source)
XLA Modules:
  0.0 233.3 jit_solution(15278113678716373417)
XLA Ops:
  7.2 1.4 pad_maximum_fusion
  8.6 1.4 broadcast_in_dim.82
  10.1 10.9 %all-to-all-start = ((bf16[16,14,512]{2,1,0:T(8,128)(2,1)}), bf16[16,14,512]{2,1,0:T(8,128)(2,1)S(1)}, u32[]{:S(2)}, u32[]{:S(2)}) async-start(bf16[16,14,512]{2,1,0:T(8,128)(2,1)} %broadcast_in_dim.82), calls=%async_computation | async-start | bytes 524288 | tf_op jit(solution)/shard_map/all_to_all | solution.py:31
  21.1 0.8 reduce-window.8
  21.9 0.7 select_reduce_fusion.1
  22.7 0.8 select_reduce_fusion
  23.7 1.0 copy.17
  24.8 1.5 fusion.18
  26.3 6.7 %all-to-all-done = bf16[16,14,512]{2,1,0:T(8,128)(2,1)S(1)} async-done(((bf16[16,14,512]{2,1,0:T(8,128)(2,1)}), bf16[16,14,512]{2,1,0:T(8,128)(2,1)S(1)}, u32[]{:S(2)}, u32[]{:S(2)}) %all-to-all-start) | async-done | bytes 229408 | tf_op jit(solution)/shard_map/all_to_all | solution.py:31
  33.0 0.8 reshape.189
  33.9 55.3 %all-gather.3.cloned.1.call-done = bf16[2048,256]{1,0:T(8,128)(2,1)} async-done(((bf16[128,256]{1,0:T(8,128)(2,1)}), bf16[2048,256]{1,0:T(8,128)(2,1)}) %all-gather.3.cloned.1.call-update) | async-done | bytes 1048592 | tf_op jit(solution)/shard_map/all_gather | solution.py:16
  89.2 1.3 fusion.41
  90.5 4.8 %while.15 = (s32[]{:T(128)}, f32[4,128]{1,0:T(4,128)S(1)}, f32[4,128]{1,0:T(4,128)S(1)}, f32[128,4,128]{0,2,1:T(8,128)S(1)}, s32[128]{0:T(128)S(1)}, /*index=5*/...) while((s32[]{:T(128)}, f32[4,128]{1,0:T(4,128)S(1)}, ...), condition=%wide.region_8.9_spmd.clone, body=%wide.region_5.8_spmd.clone.sunk | while | flops 136973312 | bytes 4371613 | solution.py:112
  90.5 0.2 compare_and_fusion.2
  90.7 0.3 fusion.55
  91.1 0.2 fusion.57
  91.3 0.4 fusion.59
  91.9 0.3 fusion.55
  92.2 0.2 fusion.57
  92.5 0.4 fusion.59
  93.1 0.3 fusion.55
  93.4 0.2 fusion.57
  93.7 0.4 fusion.59
  94.3 0.3 fusion.55
  94.6 0.2 fusion.57
  94.8 0.4 fusion.59
  95.4 34.6 %all-gather.5.cloned.1.call-done = bf16[3584,512]{1,0:T(8,128)(2,1)} async-done(((bf16[224,512]{1,0:T(8,128)(2,1)}), bf16[3584,512]{1,0:T(8,128)(2,1)}) %all-gather.5.cloned.1.call-update) | async-done | bytes 3670032 | tf_op jit(solution)/shard_map/all_gather | solution.py:123
  130.1 5.7 %convolution_convert_fusion = bf16[3584,512]{1,0:T(8,128)(2,1)} fusion(bf16[3584,512]{1,0:T(8,128)(2,1)} %all-gather.5.cloned.1.call-done, bf16[128,3584]{1,0:T(8,128)(2,1)S(1)} %copy-done, f32[128]{0:T(128)S(1)} %add_rsqrt_fusion, bf16[128,512]{1,0:T(8,128)(2,1)S(1)} %copy.22), kind=kOutput, calls=%fused_computation.27 | convolution fusion | flops 944373760 | bytes 8389120 | tf_op jit(solution)/shard_map/dot_general | solution.py:134
  135.8 67.5 %reduce-scatter.2.cloned.1.call-done = bf16[224,512]{1,0:T(8,128)(2,1)} async-done(((bf16[3584,512]{1,0:T(8,128)(2,1)}), bf16[224,512]{1,0:T(8,128)(2,1)}) %reduce-scatter.2.cloned.1.call-update) | async-done | bytes 229392 | tf_op jit(solution)/shard_map/reduce_scatter | solution.py:133
  203.2 1.0 reshape.190
  204.3 21.9 %all_to_all.10 = bf16[16,14,512]{2,1,0:T(8,128)(2,1)S(1)} all-to-all(bf16[16,14,512]{2,1,0:T(8,128)(2,1)S(1)} %reshape.190), channel_id=1, replica_groups=mesh['dp'=16,'seq'=16] {'seq'}, dimensions={0} | all-to-all | bytes 458752 | tf_op jit(solution)/shard_map/all_to_all | solution.py:45
  226.1 0.7 convert_reduce_fusion
  (45 shorter events, 1.5 us)
Async XLA Ops:
  7.2 82.0 %all-gather.3.cloned.1.call-start = ((), (), s32[]{:S(2)}) async-start(), calls=%async_computation.3 | async-start | bytes 1114112 | tf_op jit(solution)/shard_map/all_gather | solution.py:16
  10.1 22.9 %all-to-all-start = ((bf16[16,14,512]{2,1,0:T(8,128)(2,1)}), bf16[16,14,512]{2,1,0:T(8,128)(2,1)S(1)}, u32[]{:S(2)}, u32[]{:S(2)}) async-start(bf16[16,14,512]{2,1,0:T(8,128)(2,1)} %broadcast_in_dim.82), calls=%async_computation | async-start | bytes 524288 | tf_op jit(solution)/shard_map/all_to_all | solution.py:31
  21.0 109.1 %all-gather.5.cloned.1.call-start = ((), (), s32[]{:S(2)}) async-start(), calls=%async_computation.4 | async-start | bytes 3899392 | tf_op jit(solution)/shard_map/all_gather | solution.py:123
  33.8 169.4 %reduce-scatter.2.cloned.1.call-start = ((), (), s32[]{:S(2)}) async-start(), calls=%async_computation.5 | async-start | bytes 3899392 | tf_op jit(solution)/shard_map/reduce_scatter | solution.py:133
  90.5 39.6 %copy-start = (bf16[128,3584]{1,0:T(8,128)(2,1)S(1)}, bf16[128,3584]{1,0:T(8,128)(2,1)}, u32[]{:S(2)}) copy-start(bf16[128,3584]{1,0:T(8,128)(2,1)} %param.9) | copy-start | bytes 2752516
  95.4 40.3 %copy-start.1 = (bf16[128,512]{1,0:T(8,128)(2,1)}, bf16[128,512]{1,0:T(8,128)(2,1)S(1)}, u32[]{:S(2)}) copy-start(bf16[128,512]{1,0:T(8,128)(2,1)S(1)} %copy.22) | copy-start | bytes 393220
Sparse Core Ops, SparseCore 0:
  11.2 77.9 all-gather.2
  91.0 38.9 all-gather.4
  135.9 67.3 reduce-scatter.1
where the time goes:
time: 234 us; the launch traced here: 233 us
  waiting for transfers between devices  164 us (70%)
  blocking collectives  21.9 us (9%)
  between operations  13.9 us (6%)
  starting transfers between devices  11 us (5%)
  matrix products  8.39 us (4%)
  other arithmetic  7.86 us (3%)
  local copies, waits for them, and re-layouts  5.83 us (2%)
    reduce_scatter x1, waiting for transfers between devices, local(): lax.psum_scatter(lax.dot_general(columns, scaled, (((0,), (0,)), ((), ())...  67.5 us
    all_gather x1, waiting for transfers between devices, side_by_side(): lax.all_gather(both, axis, axis=dim, tiled=True)  55.3 us
    all_gather x1, waiting for transfers between devices, local(): lax.all_gather(group_rows, 'dp', axis=0, tiled=True)  34.6 us
    all_to_all x1, blocking collectives, sum_at_owner(): lax.all_to_all(tiles, axis, split_axis=0, concat_axis=0, tiled=True)  21.9 us
    all_to_all x1, starting transfers between devices, from_everyone(): return lax.all_to_all(copies, axis, split_axis=0, concat_axis=0, tiled=True)  10.9 us
    all_to_all x1, waiting for transfers between devices, from_everyone(): return lax.all_to_all(copies, axis, split_axis=0, concat_axis=0, tiled=True)  6.72 us
    dot_general x1, matrix products, local(): lax.dot_general(columns, scaled, (((0,), (0,)), ((), ())), preferred_elem...  5.65 us
  transfers between devices with their start and end apart: 4, of which 4 were waited for; matrix products, arithmetic and copies ran while one was open for 6% of the time, Pallas kernels for 0%

commit v1 on v0

--- a/solution.py
+++ b/solution.py
@@ -9,6 +9,15 @@
 BLK = 128
 EPSILON = 1e-06
 NEGATIVE = -1e30
+
+
+def work_core_by_axis(body, link_axis):
+    return jnp.concatenate(
+        lax.all_to_all(
+            jnp.stack([body for _ in range(lax.axis_size(link_axis))], axis=0), link_axis, 0, 0
+        ),
+        0,
+    )
 
 
 def side_by_side(arrays, axis, dim, along):
@@ -119,9 +128,7 @@
     group_rows = collect(weight, "seq", 0)
     columns = normed
     predicted = jnp.dot(
-        columns,
-        lax.all_gather(group_rows, "dp", axis=0, tiled=True),
-        preferred_element_type=jnp.float32,
+        columns, work_core_by_axis(group_rows, "dp"), preferred_element_type=jnp.float32
     )
     dp_count = lax.axis_size("dp")
     seq_count = lax.axis_size("seq")

time: 234 us -> 216 us (0.923)
  waiting for transfers between devices: 164 us -> 137 us
  starting transfers between devices: 11 us -> 18 us
    all_gather x1 -> x0, waiting for transfers between devices: 34.6 us -> none  [local(): lax.all_gather(group_rows, 'dp', axis=0, tiled=True)]
    all_to_all x0 -> x1, starting transfers between devices: none -> 7.04 us  [work_core_by_axis(): lax.all_to_all(jnp.stack([body for _ in range(lax.axis_size(link_axis))],...]
    all_gather x1, waiting for transfers between devices: 55.3 us -> 61.3 us  [side_by_side(): lax.all_gather(both, axis, axis=dim, tiled=True)]
  transfers between devices with their start and end apart: 4 -> 4, of which waited for: 4 -> 3; matrix products, arithmetic and copies ran while one was open for 6% -> 7% of each run, Pallas kernels for 0% -> 0%
where the time goes in v1:
time: 216 us; the launch traced here: 215 us
  waiting for transfers between devices  137 us (63%)
  blocking collectives  21.9 us (10%)
  starting transfers between devices  18 us (8%)
  between operations  14.2 us (7%)
  matrix products  8.41 us (4%)
  other arithmetic  7.86 us (4%)
  local copies, waits for them, and re-layouts  7.33 us (3%)
    reduce_scatter x1, waiting for transfers between devices, local(): lax.psum_scatter(lax.dot_general(columns, scaled, (((0,), (0,)), ((), ())...  69.2 us
    all_gather x1, waiting for transfers between devices, side_by_side(): lax.all_gather(both, axis, axis=dim, tiled=True)  61.3 us
    all_to_all x1, blocking collectives, sum_at_owner(): lax.all_to_all(tiles, axis, split_axis=0, concat_axis=0, tiled=True)  21.9 us
    all_to_all x1, starting transfers between devices, from_everyone(): return lax.all_to_all(copies, axis, split_axis=0, concat_axis=0, tiled=True)  10.9 us
    all_to_all x1, starting transfers between devices, work_core_by_axis(): lax.all_to_all(jnp.stack([body for _ in range(lax.axis_size(link_axis))],...  7.04 us
    all_to_all x1, waiting for transfers between devices, from_everyone(): return lax.all_to_all(copies, axis, split_axis=0, concat_axis=0, tiled=True)  6.74 us
    dot_general x1, matrix products, local(): lax.dot_general(columns, scaled, (((0,), (0,)), ((), ())), preferred_elem...  5.7 us
  transfers between devices with their start and end apart: 4, of which 3 were waited for; matrix products, arithmetic and copies ran while one was open for 7% of the time, Pallas kernels for 0%

profile of v1, /device:TPU:7, one launch (start us, length us, event | category | flops | bytes accessed | tf_op | source)
XLA Modules:
  0.0 215.3 jit_solution(4083643474519896397)
XLA Ops:
  7.2 1.4 pad_maximum_fusion
  8.6 1.4 broadcast_in_dim.82
  10.1 10.9 %all-to-all-start = ((bf16[16,14,512]{2,1,0:T(8,128)(2,1)}), bf16[16,14,512]{2,1,0:T(8,128)(2,1)S(1)}, u32[]{:S(2)}, u32[]{:S(2)}) async-start(bf16[16,14,512]{2,1,0:T(8,128)(2,1)} %broadcast_in_dim.82), calls=%async_computation | async-start | bytes 524288 | tf_op jit(solution)/shard_map/all_to_all | solution.py:40
  21.0 0.8 reduce-window.8
  21.9 0.8 select_reduce_fusion
  22.8 1.0 copy.17
  24.0 0.7 select_reduce_fusion.1
  24.8 1.4 fusion.18
  26.3 6.7 %all-to-all-done = bf16[16,14,512]{2,1,0:T(8,128)(2,1)S(1)} async-done(((bf16[16,14,512]{2,1,0:T(8,128)(2,1)}), bf16[16,14,512]{2,1,0:T(8,128)(2,1)S(1)}, u32[]{:S(2)}, u32[]{:S(2)}) %all-to-all-start) | async-done | bytes 229408 | tf_op jit(solution)/shard_map/all_to_all | solution.py:40
  33.1 2.2 %stack.3 = bf16[16,224,512]{2,1,0:T(8,128)(2,1)} broadcast(bf16[224,512]{1,0:T(8,128)(2,1)S(1)} %stack_reshape.2), dimensions={1,2} | broadcast | bytes 3899392 | tf_op jit(solution)/shard_map/stack | solution.py:17
  35.3 7.0 %all-to-all-start.1 = ((bf16[16,224,512]{2,1,0:T(8,128)(2,1)}), bf16[16,224,512]{2,1,0:T(8,128)(2,1)}, u32[]{:S(2)}, u32[]{:S(2)}) async-start(bf16[16,224,512]{2,1,0:T(8,128)(2,1)} %stack.3), calls=%async_computation.1 | async-start | bytes 7340032 | tf_op jit(solution)/shard_map/all_to_all | solution.py:16
  42.4 61.3 %all-gather.2.cloned.1.call-done = bf16[2048,256]{1,0:T(8,128)(2,1)} async-done(((bf16[128,256]{1,0:T(8,128)(2,1)}), bf16[2048,256]{1,0:T(8,128)(2,1)}) %all-gather.2.cloned.1.call-update) | async-done | bytes 1048592 | tf_op jit(solution)/shard_map/all_gather | solution.py:25
  103.7 1.3 fusion.41
  105.0 4.8 %while.15 = (s32[]{:T(128)}, f32[4,128]{1,0:T(4,128)S(1)}, f32[4,128]{1,0:T(4,128)S(1)}, f32[128,4,128]{0,2,1:T(8,128)S(1)}, s32[128]{0:T(128)S(1)}, /*index=5*/...) while((s32[]{:T(128)}, f32[4,128]{1,0:T(4,128)S(1)}, ...), condition=%wide.region_8.9_spmd.clone, body=%wide.region_5.8_spmd.clone.sunk | while | flops 136973312 | bytes 4371605 | solution.py:121
  105.0 0.2 compare_and_fusion.2
  105.2 0.3 fusion.55
  105.5 0.4 fusion.59
  105.9 0.2 fusion.57
  106.4 0.3 fusion.55
  106.7 0.4 fusion.59
  107.1 0.2 fusion.57
  107.6 0.3 fusion.55
  107.9 0.4 fusion.59
  108.3 0.2 fusion.57
  108.8 0.3 fusion.55
  109.1 0.4 fusion.59
  109.5 0.2 fusion.57
  109.9 5.7 %convolution_convert_fusion = bf16[3584,512]{1,0:T(8,128)(2,1)} fusion(bf16[3584,512]{1,0:T(8,128)(2,1)} %bitcast.8, bf16[128,3584]{1,0:T(8,128)(2,1)S(1)} %copy-done, f32[128]{0:T(128)S(1)} %add_rsqrt_fusion, bf16[128,512]{1,0:T(8,128)(2,1)S(1)} %copy.22), kind=kOutput, calls=%fused_computation.27 | convolution fusion | flops 944373760 | bytes 8389120 | tf_op jit(solution)/shard_map/dot_general | solution.py:141
  115.7 69.2 %reduce-scatter.2.cloned.1.call-done = bf16[224,512]{1,0:T(8,128)(2,1)} async-done(((bf16[3584,512]{1,0:T(8,128)(2,1)}), bf16[224,512]{1,0:T(8,128)(2,1)}) %reduce-scatter.2.cloned.1.call-update) | async-done | bytes 229392 | tf_op jit(solution)/shard_map/reduce_scatter | solution.py:140
  184.8 1.0 reshape.192
  185.8 21.9 %all_to_all.15 = bf16[16,14,512]{2,1,0:T(8,128)(2,1)S(1)} all-to-all(bf16[16,14,512]{2,1,0:T(8,128)(2,1)S(1)} %reshape.192), channel_id=1, replica_groups=mesh['dp'=16,'seq'=16] {'seq'}, dimensions={0} | all-to-all | bytes 458752 | tf_op jit(solution)/shard_map/all_to_all | solution.py:54
  207.8 0.7 convert_reduce_fusion
  (45 shorter events, 1.5 us)
Async XLA Ops:
  7.2 96.5 %all-gather.2.cloned.1.call-start = ((), (), s32[]{:S(2)}) async-start(), calls=%async_computation.4 | async-start | bytes 1114112 | tf_op jit(solution)/shard_map/all_gather | solution.py:25
  10.1 22.9 %all-to-all-start = ((bf16[16,14,512]{2,1,0:T(8,128)(2,1)}), bf16[16,14,512]{2,1,0:T(8,128)(2,1)S(1)}, u32[]{:S(2)}, u32[]{:S(2)}) async-start(bf16[16,14,512]{2,1,0:T(8,128)(2,1)} %broadcast_in_dim.82), calls=%async_computation | async-start | bytes 524288 | tf_op jit(solution)/shard_map/all_to_all | solution.py:40
  35.3 74.6 %all-to-all-start.1 = ((bf16[16,224,512]{2,1,0:T(8,128)(2,1)}), bf16[16,224,512]{2,1,0:T(8,128)(2,1)}, u32[]{:S(2)}, u32[]{:S(2)}) async-start(bf16[16,224,512]{2,1,0:T(8,128)(2,1)} %stack.3), calls=%async_computation.1 | async-start | bytes 7340032 | tf_op jit(solution)/shard_map/all_to_all | solution.py:16
  42.3 142.5 %reduce-scatter.2.cloned.1.call-start = ((), (), s32[]{:S(2)}) async-start(), calls=%async_computation.5 | async-start | bytes 3899392 | tf_op jit(solution)/shard_map/reduce_scatter | solution.py:140
  105.0 5.0 %copy-start = (bf16[128,3584]{1,0:T(8,128)(2,1)S(1)}, bf16[128,3584]{1,0:T(8,128)(2,1)}, u32[]{:S(2)}) copy-start(bf16[128,3584]{1,0:T(8,128)(2,1)} %param.9) | copy-start | bytes 2752516
  109.9 5.7 %copy-start.1 = (bf16[128,512]{1,0:T(8,128)(2,1)}, bf16[128,512]{1,0:T(8,128)(2,1)S(1)}, u32[]{:S(2)}) copy-start(bf16[128,512]{1,0:T(8,128)(2,1)S(1)} %copy.22) | copy-start | bytes 393220
Sparse Core Ops, SparseCore 0:
  11.2 92.4 all-gather.1
  115.8 68.9 reduce-scatter.1
